TPU v7x, 256 devices: a whole 4x4x8 slice. The times are simulated.
256 devices in a mesh: seq: 32 (over x, y, core), head: 8 (over z).
Axes of the slice: x: 4, y: 4, z: 8, core: 2. Of those that a mesh axis runs over, the one named last changes fastest.
Arguments:
- queries: bfloat16 [24576, 8192], P('seq', 'head'), may hold values from -140 to 140
- key_weight: bfloat16 [1024, 8192], P(None, 'head'), may hold values from -0.1875 to 0.1875
- value_weight: bfloat16 [1024, 8192], P(None, 'head'), may hold values from -0.1875 to 0.1875
- encodings: bfloat16 [256, 128, 1024], P('seq', None, 'head'), may hold values from -6 to 6
- nb_owner: int32 [384, 2], P('seq'), may hold values from 0 to 31, all different within a row; in each aligned block of 12 rows (0 to 11, 12 to 23, ...) at most 2 rows name the same one
- nb_block: int32 [384, 2], P('seq'), may hold values from 0 to 7
Outputs:
- attended: bfloat16 [24576, 8192], P('seq', 'head')
Inputs may be any that keep to these rules, and one draw needn't show every extreme that they name: `nb_owner`: the 2 neighbours of a span have different owners. Among the spans of one device no owner is named more than 2 times, and in every draw some device names some owner exactly 2 times.
All inputs are finite; a program needn't handle non-finite values.
Results may differ from a plain program's by a relative error of at most 0.012.
The roundings to bfloat16 on the way count: a program that leaves them out, or rounds other values in their place, can miss the bound.
Values may be sent and summed in bfloat16 or wider, within the bound.
A program may use at most 128 MiB of HBM per device.

v0:
```python
import math
import jax
import jax.numpy as jnp
from jax import lax
from jax.sharding import PartitionSpec as P

HEAD_DIM = 128
SPAN = 64


def shifted(shard, axis, by):
    devices = lax.axis_size(axis)
    pairs = [(i, i + by) for i in range(devices) if 0 <= i + by < devices]
    return lax.ppermute(shard, axis, pairs)


def on_device(queries, key_weight, value_weight, encodings, nb_owner, nb_block):
    span_dev, neighbours = nb_owner.shape
    entries = span_dev * neighbours
    db_local, block_len, slice_width = encodings.shape
    group_width = key_weight.shape[1]
    group_heads = group_width // HEAD_DIM
    peer_count = lax.axis_size("seq")
    slot_most = max(2, (entries + peer_count - 1) // peer_count)
    owner_ids = nb_owner.reshape(entries)
    block_ids = nb_block.reshape(entries)
    position = jnp.arange(entries, dtype=jnp.int32)
    same_owner = owner_ids[:, None] == owner_ids[None, :]
    before = position[None, :] < position[:, None]
    slot_ids = jnp.sum((same_owner & before).astype(jnp.int32), axis=1)
    owner_hit = owner_ids[:, None] == jnp.arange(peer_count, dtype=jnp.int32)[None, :]
    slot_hit = slot_ids[:, None] == jnp.arange(slot_most, dtype=jnp.int32)[None, :]
    marked = owner_hit[:, :, None] & slot_hit[:, None, :]
    requests = jnp.sum(jnp.where(marked, (block_ids + 1)[:, None, None], 0), axis=0)
    asked_ids = lax.all_to_all(requests, "seq", split_axis=0, concat_axis=0, tiled=True)
    present = asked_ids > 0
    picked = jnp.take(encodings, jnp.maximum(asked_ids - 1, 0), axis=0)
    picked = jnp.where(present[:, :, None, None], picked, jnp.zeros_like(picked))
    replies = lax.all_to_all(picked, "seq", split_axis=0, concat_axis=0, tiled=True)
    slot_count = replies.shape[1]
    flat_rows = replies.reshape(peer_count * slot_count, block_len, slice_width)
    compact = jnp.take(flat_rows, owner_ids * slot_count + slot_ids, axis=0)
    full_width = lax.all_gather(compact, "head", axis=2, tiled=True)
    rows = full_width.reshape(-1, full_width.shape[2])
    key_rows = jnp.dot(rows, key_weight, preferred_element_type=jnp.float32).astype(jnp.bfloat16)
    value_rows = jnp.dot(rows, value_weight, preferred_element_type=jnp.float32).astype(
        jnp.bfloat16
    )
    key_rows, value_rows = (
        key_rows.reshape(span_dev, neighbours * block_len, group_heads, HEAD_DIM),
        value_rows.reshape(span_dev, neighbours * block_len, group_heads, HEAD_DIM),
    )
    stacked = jnp.stack([key_rows[span_dev - 1], value_rows[span_dev - 1]])
    earlier = shifted(stacked, "seq", 1)
    key_rows = jnp.concatenate([earlier[0][None], key_rows], axis=0)
    value_rows = jnp.concatenate([earlier[1][None], value_rows], axis=0)
    token_count = queries.shape[0]
    grouped = jnp.pad(queries, ((1, SPAN - 1), (0, 0))).reshape(
        span_dev + 1, SPAN, group_heads, HEAD_DIM
    )
    scores = jnp.einsum(
        "cqhd,ckhd->chqk", grouped, key_rows, preferred_element_type=jnp.float32
    ) * (1.0 / math.sqrt(HEAD_DIM))
    weights = jax.nn.softmax(scores, axis=-1).astype(jnp.bfloat16)
    attended = jnp.einsum(
        "chqk,ckhd->cqhd", weights, value_rows, preferred_element_type=jnp.float32
    )
    attended = attended.reshape((span_dev + 1) * SPAN, group_width)[1 : token_count + 1]
    return attended.astype(jnp.bfloat16)


def solution(mesh):
    return jax.shard_map(
        on_device,
        mesh=mesh,
        in_specs=(
            P("seq", "head"),
            P(None, "head"),
            P(None, "head"),
            P("seq", None, "head"),
            P("seq", None),
            P("seq", None),
        ),
        out_specs=P("seq", "head"),
        check_vma=False,
    )
```

profile of v0, /device:TPU:1, one launch (start us, length us, event | category | flops | bytes accessed | tf_op | source)
XLA Modules:
  0.0 267.6 jit_solution(14205049635166241465)
XLA Ops:
  6.5 0.9 copy.63
  7.5 0.1 reshape.149
  7.5 0.2 convert_reduce_fusion
  7.7 0.1 iota_compare_fusion
  7.8 0.7 broadcast_add_fusion
  8.5 0.1 copy.64
  8.6 0.1 add.60
  8.7 0.1 select_reduce_fusion
  8.8 0.1 copy.65
  8.9 15.3 %all_to_all.14 = s32[32,1,2]{2,1,0:T(1,128)S(1)} all-to-all(s32[32,1,2]{2,1,0:T(1,128)S(1)} %copy.65), channel_id=1, replica_groups=mesh['seq'=32,'head'=8] {'seq'}, dimensions={0} | all-to-all | bytes 512 | tf_op jit(solution)/shard_map/all_to_all | solution.py:35
  24.2 0.1 copy.66
  24.3 0.1 copy.67
  24.4 0.1 copy.69
  24.5 0.1 copy.70
  24.6 0.1 reshape.158
  24.7 3.1 %gather_fusion = bf16[64,128,128]{2,1,0:T(8,128)(2,1)} fusion(bf16[8,128,128]{2,1,0:T(8,128)(2,1)} %param.9, s32[1024]{0:T(1024)S(1)} %pad_clamp_fusion.1), kind=kCustom, calls=%fused_computation | custom fusion | bytes 4194560 | tf_op jit(solution)/shard_map/jit(_take)/gather | solution.py:37
  27.8 3.3 %select_select_fusion = bf16[32,2,128,128]{3,2,1,0:T(8,128)(2,1)} fusion(bf16[32,2,128,128]{3,2,1,0:T(8,128)(2,1)} %bitcast.37, pred[32,2]{1,0:T(8,128)(4,1)S(1)} %copy.69, pred[32,2]{1,0:T(8,128)(4,1)S(1)} %copy.67), kind=kLoop, calls=%fused_computation.19 | loop fusion | flops 2097152 | bytes 4194432 | tf_op jit(solution)/shard_map/jit(_where)/select_n | solution.py:38
  31.1 5.0 %all-to-all-start.1 = ((bf16[32,2,128,128]{3,2,1,0:T(8,128)(2,1)}), bf16[32,2,128,128]{3,2,1,0:T(8,128)(2,1)}, u32[]{:S(2)}, u32[]{:S(2)}) async-start(bf16[32,2,128,128]{3,2,1,0:T(8,128)(2,1)} %select_select_fusion), calls=%async_computation.1 | async-start | bytes 4194304 | tf_op jit(solution)/shard_map/all_to_all | solution.py:39
  36.1 0.1 copy.71
  36.2 0.1 mul.25
  36.4 28.2 %all-to-all-done.1 = bf16[32,2,128,128]{3,2,1,0:T(8,128)(2,1)} async-done(((bf16[32,2,128,128]{3,2,1,0:T(8,128)(2,1)}), bf16[32,2,128,128]{3,2,1,0:T(8,128)(2,1)}, u32[]{:S(2)}, u32[]{:S(2)}) %all-to-all-start.1) | async-done | bytes 2097184 | tf_op jit(solution)/shard_map/all_to_all | solution.py:39
  64.5 2.3 gather_fusion.1
  66.8 1.0 broadcast_select_fusion
  67.9 75.7 %all-gather.2.cloned.1.call-done = bf16[24,128,1024]{2,1,0:T(8,128)(2,1)} async-done(((bf16[24,128,128]{2,1,0:T(8,128)(2,1)}), bf16[24,128,1024]{2,1,0:T(8,128)(2,1)}) %all-gather.2.cloned.1.call-update) | async-done | bytes 6291472 | tf_op jit(solution)/shard_map/all_gather | solution.py:43
  143.6 9.8 %convolution_convert_fusion.1 = bf16[3072,1024]{0,1:T(8,128)(2,1)S(1)} fusion(bf16[3072,1024]{1,0:T(8,128)(2,1)} %bitcast.44, bf16[1024,1024]{1,0:T(8,128)(2,1)S(1)} %copy-done), kind=kOutput, calls=%fused_computation.16 | convolution fusion | flops 6445596672 | bytes 14680064 | tf_op jit(solution)/shard_map/dot_general | solution.py:45
  153.4 2.6 copy-done.2
  156.0 0.1 slice.33
  156.1 0.3 copy.72
  156.4 9.5 %convolution_convert_fusion = bf16[3072,1024]{0,1:T(8,128)(2,1)S(1)} fusion(bf16[3072,1024]{1,0:T(8,128)(2,1)} %bitcast.45, bf16[1024,1024]{1,0:T(8,128)(2,1)} %param.8), kind=kOutput, calls=%fused_computation.15 | convolution fusion | flops 6445596672 | bytes 14680064 | tf_op jit(solution)/shard_map/dot_general | solution.py:46
  165.9 2.6 copy-done.3
  168.5 0.1 slice.34
  168.6 0.3 copy.73
  168.9 1.1 pad_maximum_fusion
  170.0 6.6 %collective-permute-start = (bf16[2,256,8,128]{3,1,2,0:T(8,128)(2,1)}, bf16[2,256,8,128]{3,1,2,0:T(8,128)(2,1)S(1)}, u32[]{:S(2)}, u32[]{:S(2)}) collective-permute-start(bf16[2,256,8,128]{3,1,2,0:T(8,128)(2,1)} %pad_maximum_fusion), channel_id=1, source_target_pairs={{0,8},{8,16},{16,24},{24,32},{32,40},{40,48},{48,56},{56,64},{64,7... | collective-permute-start | bytes 3145736 | tf_op jit(solution)/shard_map/ppermute | solution.py:14
  176.6 1.9 pad_bitcast_fusion
  178.5 1.7 copy.84
  180.2 12.0 %reshape.175 = bf16[12,256,8,128]{1,0,3,2:T(8,128)(2,1)} reshape(bf16[3072,1024]{0,1:T(8,128)(2,1)} %copy-done.2) | data formatting | bytes 12582912 | tf_op jit(solution)/shard_map/reshape | solution.py:50
  192.2 12.0 %reshape.174 = bf16[12,256,8,128]{1,0,3,2:T(8,128)(2,1)} reshape(bf16[3072,1024]{0,1:T(8,128)(2,1)} %copy-done.3) | data formatting | bytes 12582912 | tf_op jit(solution)/shard_map/reshape | solution.py:51
  204.3 11.9 %copy.77 = bf16[12,256,8,128]{3,1,2,0:T(8,128)(2,1)} copy(bf16[12,256,8,128]{1,0,3,2:T(8,128)(2,1)} %reshape.175) | data formatting | bytes 12582912 | tf_op jit(solution)/shard_map/reshape | solution.py:50
  216.2 12.1 %copy.75 = bf16[12,256,8,128]{3,1,2,0:T(8,128)(2,1)} copy(bf16[12,256,8,128]{1,0,3,2:T(8,128)(2,1)} %reshape.174) | data formatting | bytes 12582912 | tf_op jit(solution)/shard_map/reshape | solution.py:51
  228.3 0.9 fusion.33
  229.1 4.5 %fusion.1 = f32[13,8,64,256]{3,2,1,0:T(8,128)S(1)} fusion(bf16[12,256,8,128]{3,1,2,0:T(8,128)(2,1)} %copy.77, bf16[1,256,8,128]{3,1,2,0:T(8,128)(2,1)S(1)} %get-tuple-element.5, bf16[13,64,8,128]{3,2,1,0:T(8,128)(2,1)S(1)} %bitcast.39), kind=kOutput, calls=%fused_computation.3 | convolution fusion | flops 439615488 | bytes 15335424 | tf_op jit(solution)/shard_map/cqhd,ckhd->chqk/dot_general | solution.py:61
  233.7 2.8 %copy-done.4 = f32[13,8,64,256]{3,2,1,0:T(8,128)} copy-done((f32[13,8,64,256]{3,2,1,0:T(8,128)}, f32[13,8,64,256]{3,2,1,0:T(8,128)S(1)}, u32[]{:S(2)}) %copy-start.4) | copy-done | bytes 6815768
  236.4 2.6 fusion.34
  239.0 16.8 %fusion.18 = bf16[13,64,8,128]{3,1,2,0:T(8,128)(2,1)} fusion(bf16[12,256,8,128]{3,1,2,0:T(8,128)(2,1)} %copy.75, bf16[1,256,8,128]{3,1,2,0:T(8,128)(2,1)S(1)} %copy-done.6, f32[13,8,64]{2,1,0:T(8,128)S(1)} %fusion.34, f32[13,8,64,256]{3,2,1,0:T(8,128)} %copy-done.4), kind=kOutput, calls=%fused_computation.24 | convolution fusion | flops 459217664 | bytes 15362048 | tf_op jit(solution)/shard_map/chqk,ckhd->cqhd/dot_general | solution.py:65
  255.8 2.8 %copy.79 = bf16[13,64,8,128]{3,2,1,0:T(8,128)(2,1)S(1)} copy(bf16[13,64,8,128]{3,1,2,0:T(8,128)(2,1)} %fusion.18) | data formatting | bytes 3407872 | tf_op jit(solution)/shard_map/chqk,ckhd->cqhd/transpose | solution.py:65
  258.6 0.5 copy.89
  259.1 1.6 slice.37
  (24 shorter events, 0.1 us)
Async XLA Ops:
  6.5 137.0 %copy-start = (bf16[1024,1024]{1,0:T(8,128)(2,1)S(1)}, bf16[1024,1024]{1,0:T(8,128)(2,1)}, u32[]{:S(2)}) copy-start(bf16[1024,1024]{1,0:T(8,128)(2,1)} %param.7) | copy-start | bytes 6291460
  24.7 11.4 %copy-start.7 = (s32[12,2]{0,1:T(2,128)S(1)}, s32[12,2]{0,1:T(2,128)}, u32[]{:S(2)}) copy-start(s32[12,2]{0,1:T(2,128)} %param.10) | copy-start | bytes 292
  31.1 33.5 %all-to-all-start.1 = ((bf16[32,2,128,128]{3,2,1,0:T(8,128)(2,1)}), bf16[32,2,128,128]{3,2,1,0:T(8,128)(2,1)}, u32[]{:S(2)}, u32[]{:S(2)}) async-start(bf16[32,2,128,128]{3,2,1,0:T(8,128)(2,1)} %select_select_fusion), calls=%async_computation.1 | async-start | bytes 4194304 | tf_op jit(solution)/shard_map/all_to_all | solution.py:39
  36.1 107.5 %all-gather.2.cloned.1.call-start = ((), (), s32[]{:S(2)}) async-start(), calls=%async_computation.2 | async-start | bytes 7077888 | tf_op jit(solution)/shard_map/all_gather | solution.py:43
  153.4 2.7 copy-start.2
  165.9 2.6 copy-start.3
  170.0 58.3 %collective-permute-start = (bf16[2,256,8,128]{3,1,2,0:T(8,128)(2,1)}, bf16[2,256,8,128]{3,1,2,0:T(8,128)(2,1)S(1)}, u32[]{:S(2)}, u32[]{:S(2)}) collective-permute-start(bf16[2,256,8,128]{3,1,2,0:T(8,128)(2,1)} %pad_maximum_fusion), channel_id=1, source_target_pairs={{0,8},{8,16},{16,24},{24,32},{32,40},{40,48},{48,56},{56,64},{64,7... | collective-permute-start | bytes 3145736 | tf_op jit(solution)/shard_map/ppermute | solution.py:14
  216.2 13.0 %copy-start.5 = (bf16[104,8,8,128]{3,2,1,0:T(8,128)(2,1)S(1)}, bf16[104,8,8,128]{3,2,1,0:T(8,128)(2,1)}, u32[]{:S(2)}) copy-start(bf16[104,8,8,128]{3,2,1,0:T(8,128)(2,1)} %copy.84) | copy-start | bytes 5111812
  233.6 2.8 %copy-start.4 = (f32[13,8,64,256]{3,2,1,0:T(8,128)}, f32[13,8,64,256]{3,2,1,0:T(8,128)S(1)}, u32[]{:S(2)}) copy-start(f32[13,8,64,256]{3,2,1,0:T(8,128)S(1)} %fusion.1) | copy-start | bytes 20447236
  236.4 2.6 copy-start.6
  239.0 21.7 %copy-start.1 = (bf16[1024,1024]{1,0:T(8,128)(2,1)S(1)}, bf16[1024,1024]{1,0:T(8,128)(2,1)}, u32[]{:S(2)}) copy-start(bf16[1024,1024]{1,0:T(8,128)(2,1)} %param.7) | copy-start | bytes 6291460
Sparse Core Ops, SparseCore 0:
  68.0 75.5 all-gather.1
where the time goes:
time: 269 us; the launch traced here: 268 us
  waiting for transfers between devices  104 us (39%)
  local copies, waits for them, and re-layouts  73.5 us (27%)
  matrix products  40.6 us (15%)
  blocking collectives  15.3 us (6%)
  between operations  13.6 us (5%)
  starting transfers between devices  11.6 us (4%)
  other arithmetic  9.01 us (3%)
    all_gather x1, waiting for transfers between devices, on_device(): full_width = lax.all_gather(compact, 'head', axis=2, tiled=True)  75.7 us
    all_to_all x1, waiting for transfers between devices, on_device(): lax.all_to_all(picked, 'seq', split_axis=0, concat_axis=0, tiled=True)  28.2 us
    reshape x2, local copies, waits for them, and re-layouts, on_device(): value_rows.reshape(span_dev, neighbours * block_len, group_heads, HEAD_DIM)  24.1 us
    reshape x2, local copies, waits for them, and re-layouts, on_device(): key_rows.reshape(span_dev, neighbours * block_len, group_heads, HEAD_DIM)  23.9 us
    dot_general x1, matrix products, on_device(): jnp.einsum('chqk,ckhd->cqhd', weights, value_rows, preferred_element_type...  16.8 us
    all_to_all x1, blocking collectives, on_device(): lax.all_to_all(requests, 'seq', split_axis=0, concat_axis=0, tiled=True)  15.3 us
    unnamed x20, local copies, waits for them, and re-layouts  13.1 us
    dot_general x1, matrix products, on_device(): jnp.dot(rows, key_weight, preferred_element_type=jnp.float32)  9.79 us
  transfers between devices with their start and end apart: 3, of which 2 were waited for; matrix products, arithmetic and copies ran while one was open for 19% of the time, Pallas kernels for 0%

commit v1 on v0

--- a/solution.py
+++ b/solution.py
@@ -40,7 +40,19 @@
     slot_count = replies.shape[1]
     flat_rows = replies.reshape(peer_count * slot_count, block_len, slice_width)
     compact = jnp.take(flat_rows, owner_ids * slot_count + slot_ids, axis=0)
-    full_width = lax.all_gather(compact, "head", axis=2, tiled=True)
+    how_many = lax.axis_size("head")
+    vals = [(dev_j, (dev_j + 1) % how_many) for dev_j in range(how_many)]
+    line_up = [(dev_j, (dev_j - 1) % how_many) for dev_j in range(how_many)]
+    oldest, val = ([compact], [compact])
+    for _ in range(how_many // 2):
+        oldest.append(lax.ppermute(oldest[-1], "head", vals))
+    for _ in range((how_many - 1) // 2):
+        val.append(lax.ppermute(val[-1], "head", line_up))
+    full_width = jnp.roll(
+        jnp.concatenate([*oldest[::-1], *val[1:]], axis=2),
+        shift=(lax.axis_index("head") - how_many // 2) * compact.shape[2],
+        axis=2,
+    )
     rows = full_width.reshape(-1, full_width.shape[2])
     key_rows = jnp.dot(rows, key_weight, preferred_element_type=jnp.float32).astype(jnp.bfloat16)
     value_rows = jnp.dot(rows, value_weight, preferred_element_type=jnp.float32).astype(

time: 269 us -> 288 us (1.071)
  local copies, waits for them, and re-layouts: 73.5 us -> 105 us
  between operations: 13.6 us -> 0.26 us
  waiting for transfers between devices: 104 us -> 95.8 us
  starting transfers between devices: 11.6 us -> 19.4 us
    all_gather x1 -> x0, waiting for transfers between devices: 75.7 us -> none  [on_device(): full_width = lax.all_gather(compact, 'head', axis=2, tiled=True)]
    ppermute x0 -> x7, waiting for transfers between devices: none -> 67.6 us  [the longest x4 67.6 us: on_device(): oldest.append(lax.ppermute(oldest[-1], 'head', vals))]
    unnamed x20 -> x43, local copies, waits for them, and re-layouts: 13.1 us -> 39.8 us
    ppermute x0 -> x7, starting transfers between devices: none -> 9.74 us  [the longest x3 8.02 us: on_device(): val.append(lax.ppermute(val[-1], 'head', line_up))]
    dynamic_slice x0 -> x1, local copies, waits for them, and re-layouts: none -> 3.49 us  [on_device(): jnp.roll(jnp.concatenate([*oldest[::-1], *val[1:]], axis=2), shift=(lax.a...]
  transfers between devices with their start and end apart: 3 -> 9, of which waited for: 2 -> 5; matrix products, arithmetic and copies ran while one was open for 19% -> 23% of each run, Pallas kernels for 0% -> 0%
where the time goes in v1:
time: 288 us; the launch traced here: 284 us
  local copies, waits for them, and re-layouts  105 us (36%)
  waiting for transfers between devices  95.8 us (33%)
  matrix products  38.1 us (13%)
  starting transfers between devices  19.4 us (7%)
  blocking collectives  15.3 us (5%)
  other arithmetic  10.5 us (4%)
    ppermute x4, waiting for transfers between devices, on_device(): oldest.append(lax.ppermute(oldest[-1], 'head', vals))  67.6 us
    unnamed x43, local copies, waits for them, and re-layouts  39.8 us
    all_to_all x1, waiting for transfers between devices, on_device(): lax.all_to_all(picked, 'seq', split_axis=0, concat_axis=0, tiled=True)  28.2 us
    reshape x2, local copies, waits for them, and re-layouts, on_device(): value_rows.reshape(span_dev, neighbours * block_len, group_heads, HEAD_DIM)  24.1 us
    reshape x2, local copies, waits for them, and re-layouts, on_device(): key_rows.reshape(span_dev, neighbours * block_len, group_heads, HEAD_DIM)  24 us
    dot_general x1, matrix products, on_device(): jnp.einsum('chqk,ckhd->cqhd', weights, value_rows, preferred_element_type...  16.8 us
    all_to_all x1, blocking collectives, on_device(): lax.all_to_all(requests, 'seq', split_axis=0, concat_axis=0, tiled=True)  15.3 us
    dot_general x1, matrix products, on_device(): jnp.dot(rows, value_weight, preferred_element_type=jnp.float32)  9.52 us
  transfers between devices with their start and end apart: 9, of which 5 were waited for; matrix products, arithmetic and copies ran while one was open for 23% of the time, Pallas kernels for 0%

profile of v1, /device:TPU:1, one launch (start us, length us, event | category | flops | bytes accessed | tf_op | source)
XLA Modules:
  0.0 284.2 jit_solution(15865549955243313030)
XLA Ops:
  2.3 15.3 %all_to_all.14 = s32[32,1,2]{2,1,0:T(1,128)S(1)} all-to-all(s32[32,1,2]{2,1,0:T(1,128)S(1)} %copy.65), channel_id=1, replica_groups=mesh['seq'=32,'head'=8] {'seq'}, dimensions={0} | all-to-all | bytes 512 | tf_op jit(solution)/shard_map/all_to_all | solution.py:35
  18.2 3.1 %gather_fusion = bf16[64,128,128]{2,1,0:T(8,128)(2,1)} fusion(bf16[8,128,128]{2,1,0:T(8,128)(2,1)} %param.9, s32[1024]{0:T(1024)S(1)} %pad_clamp_fusion.1), kind=kCustom, calls=%fused_computation | custom fusion | bytes 4194560 | tf_op jit(solution)/shard_map/jit(_take)/gather | solution.py:37
  21.3 3.2 %select_select_fusion = bf16[32,2,128,128]{3,2,1,0:T(8,128)(2,1)} fusion(bf16[32,2,128,128]{3,2,1,0:T(8,128)(2,1)} %bitcast.37, pred[32,2]{1,0:T(8,128)(4,1)S(1)} %copy.69, pred[32,2]{1,0:T(8,128)(4,1)S(1)} %copy.67), kind=kLoop, calls=%fused_computation.19 | loop fusion | flops 2097152 | bytes 4194432 | tf_op jit(solution)/shard_map/jit(_where)/select_n | solution.py:38
  24.5 5.0 %all-to-all-start.1 = ((bf16[32,2,128,128]{3,2,1,0:T(8,128)(2,1)}), bf16[32,2,128,128]{3,2,1,0:T(8,128)(2,1)}, u32[]{:S(2)}, u32[]{:S(2)}) async-start(bf16[32,2,128,128]{3,2,1,0:T(8,128)(2,1)} %select_select_fusion), calls=%async_computation.1 | async-start | bytes 4194304 | tf_op jit(solution)/shard_map/all_to_all | solution.py:39
  29.8 28.2 %all-to-all-done.1 = bf16[32,2,128,128]{3,2,1,0:T(8,128)(2,1)} async-done(((bf16[32,2,128,128]{3,2,1,0:T(8,128)(2,1)}), bf16[32,2,128,128]{3,2,1,0:T(8,128)(2,1)}, u32[]{:S(2)}, u32[]{:S(2)}) %all-to-all-start.1) | async-done | bytes 2097184 | tf_op jit(solution)/shard_map/all_to_all | solution.py:39
  58.0 2.3 gather_fusion.1
  60.5 1.7 collective-permute-start
  62.2 21.0 %collective-permute-done = bf16[24,128,128]{2,1,0:T(8,128)(2,1)S(1)} collective-permute-done((bf16[24,128,128]{2,1,0:T(8,128)(2,1)S(1)}, bf16[24,128,128]{2,1,0:T(8,128)(2,1)S(1)}, u32[]{:S(2)}, u32[]{:S(2)}) %collective-permute-start) | collective-permute-done | bytes 786464 | tf_op jit(solution)/shard_map/ppermute | solution.py:48
  84.1 2.7 collective-permute-start.4
  86.8 16.2 %collective-permute-done.1 = bf16[24,128,128]{2,1,0:T(8,128)(2,1)S(1)} collective-permute-done((bf16[24,128,128]{2,1,0:T(8,128)(2,1)S(1)}, bf16[24,128,128]{2,1,0:T(8,128)(2,1)S(1)}, u32[]{:S(2)}, u32[]{:S(2)}) %collective-permute-start.1) | collective-permute-done | bytes 786464 | tf_op jit(solution)/shard_map/ppermute | solution.py:48
  103.9 2.7 collective-permute-start.5
  106.6 15.5 %collective-permute-done.2 = bf16[24,128,128]{2,1,0:T(8,128)(2,1)} collective-permute-done((bf16[24,128,128]{2,1,0:T(8,128)(2,1)S(1)}, bf16[24,128,128]{2,1,0:T(8,128)(2,1)}, u32[]{:S(2)}, u32[]{:S(2)}) %collective-permute-start.2) | collective-permute-done | bytes 786464 | tf_op jit(solution)/shard_map/ppermute | solution.py:48
  122.1 2.7 collective-permute-start.6
  124.8 14.8 %collective-permute-done.3 = bf16[24,128,128]{2,1,0:T(8,128)(2,1)} collective-permute-done((bf16[24,128,128]{2,1,0:T(8,128)(2,1)}, bf16[24,128,128]{2,1,0:T(8,128)(2,1)}, u32[]{:S(2)}, u32[]{:S(2)}) %collective-permute-start.3) | collective-permute-done | bytes 786464 | tf_op jit(solution)/shard_map/ppermute | solution.py:48
  139.6 2.1 constant_dynamic-update-slice_fusion.15
  141.8 2.2 constant_dynamic-update-slice_fusion.14
  144.0 2.2 constant_dynamic-update-slice_fusion.13
  146.2 2.2 constant_dynamic-update-slice_fusion.12
  148.4 1.2 constant_dynamic-update-slice_fusion.11
  149.6 2.2 constant_dynamic-update-slice_fusion.10
  151.8 2.1 constant_dynamic-update-slice_fusion.9
  154.9 2.2 constant_dynamic-update-slice_fusion.7
  157.1 2.2 constant_dynamic-update-slice_fusion.6
  159.3 1.0 constant_dynamic-update-slice_fusion.5
  160.4 1.0 constant_dynamic-update-slice_fusion.4
  161.4 1.2 constant_dynamic-update-slice_fusion.3
  162.5 2.2 constant_dynamic-update-slice_fusion.2
  164.7 2.2 constant_dynamic-update-slice_fusion.1
  166.8 1.0 constant_dynamic-update-slice_fusion
  167.8 3.5 %constant_dynamic-slice_fusion = bf16[24,128,1024]{2,1,0:T(8,128)(2,1)S(1)} fusion(bf16[24,128,2048]{2,1,0:T(8,128)(2,1)} %constant_dynamic-update-slice_fusion, s32[]{:T(128)S(6)} %select_n.55), kind=kLoop, calls=%fused_computation.62 | loop fusion | bytes 12582916 | tf_op jit(solution)/shard_map/jit(_roll_dynamic)/dynamic_slice | solution.py:51
  171.3 7.3 %convolution_convert_fusion.1 = bf16[3072,1024]{0,1:T(8,128)(2,1)S(1)} fusion(bf16[3072,1024]{1,0:T(8,128)(2,1)S(1)} %bitcast.41, bf16[1024,1024]{1,0:T(8,128)(2,1)S(1)} %copy-done), kind=kOutput, calls=%fused_computation.16 | convolution fusion | flops 6445596672 | bytes 14680064 | tf_op jit(solution)/shard_map/dot_general | solution.py:57
  178.7 2.7 copy-done.2
  181.7 9.5 %convolution_convert_fusion = bf16[3072,1024]{0,1:T(8,128)(2,1)S(1)} fusion(bf16[3072,1024]{1,0:T(8,128)(2,1)} %bitcast.42, bf16[1024,1024]{1,0:T(8,128)(2,1)} %param.8), kind=kOutput, calls=%fused_computation.15 | convolution fusion | flops 6445596672 | bytes 14680064 | tf_op jit(solution)/shard_map/dot_general | solution.py:58
  191.2 2.6 copy-done.3
  194.2 1.1 pad_maximum_fusion
  195.3 4.6 %collective-permute-start.7 = (bf16[2,256,8,128]{3,1,2,0:T(8,128)(2,1)}, bf16[2,256,8,128]{3,1,2,0:T(8,128)(2,1)S(1)}, u32[]{:S(2)}, u32[]{:S(2)}) collective-permute-start(bf16[2,256,8,128]{3,1,2,0:T(8,128)(2,1)} %pad_maximum_fusion), channel_id=1, source_target_pairs={{0,8},{8,16},{16,24},{24,32},{32,40},{40,48},{48,56},{56,64},{64,7... | collective-permute-start | bytes 3145736 | tf_op jit(solution)/shard_map/ppermute | solution.py:14
  199.9 1.9 pad_bitcast_fusion
  201.8 1.7 copy.84
  203.5 12.0 %reshape.175 = bf16[12,256,8,128]{1,0,3,2:T(8,128)(2,1)} reshape(bf16[3072,1024]{0,1:T(8,128)(2,1)} %copy-done.2) | data formatting | bytes 12582912 | tf_op jit(solution)/shard_map/reshape | solution.py:62
  215.6 12.1 %reshape.174 = bf16[12,256,8,128]{1,0,3,2:T(8,128)(2,1)} reshape(bf16[3072,1024]{0,1:T(8,128)(2,1)} %copy-done.3) | data formatting | bytes 12582912 | tf_op jit(solution)/shard_map/reshape | solution.py:63
  227.7 11.9 %copy.77 = bf16[12,256,8,128]{3,1,2,0:T(8,128)(2,1)} copy(bf16[12,256,8,128]{1,0,3,2:T(8,128)(2,1)} %reshape.175) | data formatting | bytes 12582912 | tf_op jit(solution)/shard_map/reshape | solution.py:62
  239.6 12.1 %copy.75 = bf16[12,256,8,128]{3,1,2,0:T(8,128)(2,1)} copy(bf16[12,256,8,128]{1,0,3,2:T(8,128)(2,1)} %reshape.174) | data formatting | bytes 12582912 | tf_op jit(solution)/shard_map/reshape | solution.py:63
  252.5 4.5 %fusion.1 = f32[13,8,64,256]{3,2,1,0:T(8,128)S(1)} fusion(bf16[12,256,8,128]{3,1,2,0:T(8,128)(2,1)} %copy.77, bf16[1,256,8,128]{3,1,2,0:T(8,128)(2,1)S(1)} %get-tuple-element.5, bf16[13,64,8,128]{3,2,1,0:T(8,128)(2,1)S(1)} %bitcast.39), kind=kOutput, calls=%fused_computation.3 | convolution fusion | flops 439615488 | bytes 15335424 | tf_op jit(solution)/shard_map/cqhd,ckhd->chqk/dot_general | solution.py:73
  257.1 2.8 copy-done.4
  259.9 2.6 fusion.34
  262.5 16.8 %fusion.18 = bf16[13,64,8,128]{3,1,2,0:T(8,128)(2,1)} fusion(bf16[12,256,8,128]{3,1,2,0:T(8,128)(2,1)} %copy.75, bf16[1,256,8,128]{3,1,2,0:T(8,128)(2,1)S(1)} %copy-done.11, f32[13,8,64]{2,1,0:T(8,128)S(1)} %fusion.34, f32[13,8,64,256]{3,2,1,0:T(8,128)} %copy-done.4), kind=kOutput, calls=%fused_computation.24 | convolution fusion | flops 459217664 | bytes 15362048 | tf_op jit(solution)/shard_map/chqk,ckhd->cqhd/dot_general | solution.py:77
  279.3 2.8 copy.79
  282.6 1.6 slice.37
  (62 shorter events, 8.0 us)
Async XLA Ops:
  0.0 171.3 %copy-start = (bf16[1024,1024]{1,0:T(8,128)(2,1)S(1)}, bf16[1024,1024]{1,0:T(8,128)(2,1)}, u32[]{:S(2)}) copy-start(bf16[1024,1024]{1,0:T(8,128)(2,1)} %param.7) | copy-start | bytes 6291460
  0.0 29.6 %copy-start.12 = (s32[12,2]{0,1:T(2,128)S(1)}, s32[12,2]{0,1:T(2,128)}, u32[]{:S(2)}) copy-start(s32[12,2]{0,1:T(2,128)} %param.10) | copy-start | bytes 292
  24.5 33.5 %all-to-all-start.1 = ((bf16[32,2,128,128]{3,2,1,0:T(8,128)(2,1)}), bf16[32,2,128,128]{3,2,1,0:T(8,128)(2,1)}, u32[]{:S(2)}, u32[]{:S(2)}) async-start(bf16[32,2,128,128]{3,2,1,0:T(8,128)(2,1)} %select_select_fusion), calls=%async_computation.1 | async-start | bytes 4194304 | tf_op jit(solution)/shard_map/all_to_all | solution.py:39
  60.5 22.8 %collective-permute-start = (bf16[24,128,128]{2,1,0:T(8,128)(2,1)S(1)}, bf16[24,128,128]{2,1,0:T(8,128)(2,1)S(1)}, u32[]{:S(2)}, u32[]{:S(2)}) collective-permute-start(bf16[24,128,128]{2,1,0:T(8,128)(2,1)S(1)} %broadcast_select_fusion), channel_id=1, source_target_pairs={{0,1},{1,2},{2,3},{3,4},{4,5},{5,6},{6,7},{7,0},{8,9},{9,10},{10,1... | collective-permute-start | bytes 2359304 | tf_op jit(solution)/shard_map/ppermute | solution.py:48
  83.2 0.9 copy-start.7
  84.1 18.9 %collective-permute-start.1 = (bf16[24,128,128]{2,1,0:T(8,128)(2,1)S(1)}, bf16[24,128,128]{2,1,0:T(8,128)(2,1)S(1)}, u32[]{:S(2)}, u32[]{:S(2)}) collective-permute-start(bf16[24,128,128]{2,1,0:T(8,128)(2,1)S(1)} %collective-permute-done), channel_id=1, source_target_pairs={{0,1},{1,2},{2,3},{3,4},{4,5},{5,6},{6,7},{7,0},{8,9},{9,10},{10,1... | collective-permute-start | bytes 2359304 | tf_op jit(solution)/shard_map/ppermute | solution.py:48
  84.1 19.8 %collective-permute-start.4 = (bf16[24,128,128]{2,1,0:T(8,128)(2,1)S(1)}, bf16[24,128,128]{2,1,0:T(8,128)(2,1)}, u32[]{:S(2)}, u32[]{:S(2)}) collective-permute-start(bf16[24,128,128]{2,1,0:T(8,128)(2,1)S(1)} %broadcast_select_fusion), channel_id=1, source_target_pairs={{0,7},{1,0},{2,1},{3,2},{4,3},{5,4},{6,5},{7,6},{8,15},{9,8},{10,9... | collective-permute-start | bytes 2359304 | tf_op jit(solution)/shard_map/ppermute | solution.py:50
  103.0 0.9 copy-start.9
  103.9 18.2 %collective-permute-start.2 = (bf16[24,128,128]{2,1,0:T(8,128)(2,1)S(1)}, bf16[24,128,128]{2,1,0:T(8,128)(2,1)}, u32[]{:S(2)}, u32[]{:S(2)}) collective-permute-start(bf16[24,128,128]{2,1,0:T(8,128)(2,1)S(1)} %collective-permute-done.1), channel_id=1, source_target_pairs={{0,1},{1,2},{2,3},{3,4},{4,5},{5,6},{6,7},{7,0},{8,9},{9,10},{10,1... | collective-permute-start | bytes 2359304 | tf_op jit(solution)/shard_map/ppermute | solution.py:48
  103.9 18.2 %collective-permute-start.5 = (bf16[24,128,128]{2,1,0:T(8,128)(2,1)}, bf16[24,128,128]{2,1,0:T(8,128)(2,1)}, u32[]{:S(2)}, u32[]{:S(2)}) collective-permute-start(bf16[24,128,128]{2,1,0:T(8,128)(2,1)} %collective-permute-done.4), channel_id=1, source_target_pairs={{0,7},{1,0},{2,1},{3,2},{4,3},{5,4},{6,5},{7,6},{8,15},{9,8},{10,9... | collective-permute-start | bytes 2359304 | tf_op jit(solution)/shard_map/ppermute | solution.py:50
  122.1 17.5 %collective-permute-start.3 = (bf16[24,128,128]{2,1,0:T(8,128)(2,1)}, bf16[24,128,128]{2,1,0:T(8,128)(2,1)}, u32[]{:S(2)}, u32[]{:S(2)}) collective-permute-start(bf16[24,128,128]{2,1,0:T(8,128)(2,1)} %collective-permute-done.2), channel_id=1, source_target_pairs={{0,1},{1,2},{2,3},{3,4},{4,5},{5,6},{6,7},{7,0},{8,9},{9,10},{10,1... | collective-permute-start | bytes 2359304 | tf_op jit(solution)/shard_map/ppermute | solution.py:48
  122.1 31.8 %collective-permute-start.6 = (bf16[24,128,128]{2,1,0:T(8,128)(2,1)}, bf16[24,128,128]{2,1,0:T(8,128)(2,1)S(1)}, u32[]{:S(2)}, u32[]{:S(2)}) collective-permute-start(bf16[24,128,128]{2,1,0:T(8,128)(2,1)} %collective-permute-done.5), channel_id=1, source_target_pairs={{0,7},{1,0},{2,1},{3,2},{4,3},{5,4},{6,5},{7,6},{8,15},{9,8},{10,9... | collective-permute-start | bytes 2359304 | tf_op jit(solution)/shard_map/ppermute | solution.py:50
  141.7 17.6 %copy-start.10 = (bf16[24,128,128]{2,1,0:T(8,128)(2,1)S(1)}, bf16[24,128,128]{2,1,0:T(8,128)(2,1)}, u32[]{:S(2)}) copy-start(bf16[24,128,128]{2,1,0:T(8,128)(2,1)} %copy-done.9) | copy-start | bytes 2359300
  144.0 16.4 %copy-start.8 = (bf16[24,128,128]{2,1,0:T(8,128)(2,1)S(1)}, bf16[24,128,128]{2,1,0:T(8,128)(2,1)}, u32[]{:S(2)}) copy-start(bf16[24,128,128]{2,1,0:T(8,128)(2,1)} %copy-done.7) | copy-start | bytes 2359300
  171.3 7.3 %copy-start.6 = (bf16[24,128,1024]{2,1,0:T(8,128)(2,1)}, bf16[24,128,1024]{2,1,0:T(8,128)(2,1)S(1)}, u32[]{:S(2)}) copy-start(bf16[24,128,1024]{2,1,0:T(8,128)(2,1)S(1)} %constant_dynamic-slice_fusion) | copy-start | bytes 18874372
  178.7 2.7 copy-start.2
  191.2 2.7 copy-start.3
  195.3 56.4 %collective-permute-start.7 = (bf16[2,256,8,128]{3,1,2,0:T(8,128)(2,1)}, bf16[2,256,8,128]{3,1,2,0:T(8,128)(2,1)S(1)}, u32[]{:S(2)}, u32[]{:S(2)}) collective-permute-start(bf16[2,256,8,128]{3,1,2,0:T(8,128)(2,1)} %pad_maximum_fusion), channel_id=1, source_target_pairs={{0,8},{8,16},{16,24},{24,32},{32,40},{40,48},{48,56},{56,64},{64,7... | collective-permute-start | bytes 3145736 | tf_op jit(solution)/shard_map/ppermute | solution.py:14
  239.6 12.9 %copy-start.5 = (bf16[104,8,8,128]{3,2,1,0:T(8,128)(2,1)S(1)}, bf16[104,8,8,128]{3,2,1,0:T(8,128)(2,1)}, u32[]{:S(2)}) copy-start(bf16[104,8,8,128]{3,2,1,0:T(8,128)(2,1)} %copy.84) | copy-start | bytes 5111812
  257.0 2.8 copy-start.4
  259.9 2.6 copy-start.11
  262.5 21.7 %copy-start.1 = (bf16[1024,1024]{1,0:T(8,128)(2,1)S(1)}, bf16[1024,1024]{1,0:T(8,128)(2,1)}, u32[]{:S(2)}) copy-start(bf16[1024,1024]{1,0:T(8,128)(2,1)} %param.7) | copy-start | bytes 6291460
